TPU v7x, 128 devices: a whole 4x4x4 slice. The times are simulated.
128 devices in a mesh: seq: 8 (over y, core), tile: 16 (over z, x).
Axes of the slice: x: 4, y: 4, z: 4, core: 2. Of those that a mesh axis runs over, the one named last changes fastest.
Arguments:
- latents: bfloat16 [16384, 128], P(('seq', 'tile')), may hold values from -6 to 6
- grid_slot: int32 [16384], P(('seq', 'tile')), may hold values from 0 to 16383, as said below
- w_in: bfloat16 [432, 384], replicated, may hold values from -0.3125 to 0.3125
- b_in: float32 [384], replicated, may hold values from -3 to 3
- gain_in: float32 [384], replicated, may hold values from 0.1 to 1.9
- w_up: bfloat16 [3456, 192], replicated, may hold values from -0.109375 to 0.109375
- b_up: float32 [192], replicated, may hold values from -3 to 3
- gain_res: float32 [192], replicated, may hold values from 0.1 to 1.9
- w_res: bfloat16 [5184, 192], replicated, may hold values from -0.078125 to 0.078125
- b_res: float32 [192], replicated, may hold values from -3 to 3
Outputs:
- decoded: bfloat16 [16, 128, 49152], P(None, 'tile', 'seq')
Inputs may be any that keep to these rules, and one draw needn't show every extreme that they name: grid_slot is a permutation of 0 to 16383. Row r of the sequence lies on device r // 128 and grid row p on device p // 128 (devices in the order seq then tile). The rows of one device go to exactly 64 receiving devices, exactly 2 rows to each, so every device receives 128 rows; the receivers of device d are d + k modulo 128 for a set of offsets k common to all devices, which includes 128 / 2.
All inputs are finite; a program needn't handle non-finite values.
Results may differ from a plain program's by a relative error of at most 0.0058.
Values may be sent and summed in bfloat16 or wider, within the bound.
No kernel may reach another device: no remote copies, remote signals or barrier semaphores. Data moves between devices by JAX's collectives and lax.ppermute only.
A program may use at most 192 MiB of HBM per device.

v0:
```python
import jax
import jax.numpy as jnp
from jax import lax
from jax.sharding import PartitionSpec as P

LAT = 16
C1 = 384
C2 = 192
FS = 2
TH = 4
W = 128


def extended_2(block, sides, width):
    for axis, dim in sides:
        count = lax.axis_size(axis)
        forward = [(i, i + 1) for i in range(count - 1)]
        backward = [(target, source) for source, target in forward]
        low = lax.ppermute(
            lax.slice_in_dim(block, block.shape[dim] - width, None, axis=dim), axis, forward
        )
        high = lax.ppermute(lax.slice_in_dim(block, 0, width, axis=dim), axis, backward)
        block = jnp.concatenate([low, block, high], axis=dim)
    return block


def from_behind(x, axis, by):
    length = lax.axis_size(axis)
    pairs = [(i, i + by) for i in range(length) if 0 <= i + by < length]
    return lax.ppermute(x, axis, pairs)


def causal_taps(padded, weight, bias):
    frames = padded.shape[0] - 2
    height = padded.shape[1] - 2
    breadth = padded.shape[2] - 2
    channels = padded.shape[3]
    running = jnp.zeros((frames * height * breadth, weight.shape[1]), jnp.float32)
    for time_off in range(3):
        for row_off in range(3):
            window = jnp.concatenate(
                [
                    padded[
                        time_off : time_off + frames,
                        row_off : row_off + height,
                        col_off : col_off + breadth,
                    ]
                    for col_off in range(3)
                ],
                axis=-1,
            )
            start = (time_off * 3 + row_off) * 3 * channels
            running = running + jnp.dot(
                window.reshape(-1, 3 * channels),
                weight[start : start + 3 * channels],
                preferred_element_type=jnp.float32,
            )
    return (running + bias).reshape(frames, height, breadth, weight.shape[1])


def upsample_conv(extended, weight, bias):
    doubled = jnp.repeat(jnp.repeat(extended, 2, axis=1), 2, axis=2)[:, 1:-1, 1:-1]
    frames = doubled.shape[0]
    height = doubled.shape[1] - 2
    breadth = doubled.shape[2] - 2
    channels = doubled.shape[3]
    running = jnp.zeros((frames * height * breadth, weight.shape[1]), jnp.float32)
    for row_off in range(3):
        window = jnp.concatenate(
            [
                doubled[:, row_off : row_off + height, col_off : col_off + breadth]
                for col_off in range(3)
            ],
            axis=-1,
        )
        start = row_off * 3 * channels
        running = running + jnp.dot(
            window.reshape(-1, 3 * channels),
            weight[start : start + 3 * channels],
            preferred_element_type=jnp.float32,
        )
    return (running + bias).astype(jnp.bfloat16).reshape(frames, height, breadth, weight.shape[1])


def normed_silu(values, gain):
    scaled = values * lax.rsqrt(jnp.mean(values * values, axis=-1, keepdims=True) + 1e-06) * gain
    return jax.nn.silu(scaled).astype(jnp.bfloat16)


def local(latents, grid_slot, w_in, b_in, gain_in, w_up, b_up, gain_res, w_res, b_res):
    seq_count = lax.axis_size("seq")
    tile_count = lax.axis_size("tile")
    device_count = seq_count * tile_count
    row_count = latents.shape[0]
    row_width = latents.shape[1]
    slot_cap = 2 * row_count // device_count
    target = grid_slot // row_count
    local_row = grid_slot % row_count
    one_hot = (target[:, None] == jnp.arange(device_count, dtype=jnp.int32)[None, :]).astype(
        jnp.int32
    )
    rank_in = jnp.sum((jnp.cumsum(one_hot, axis=0) - 1) * one_hot, axis=1)
    send_slot = target * slot_cap + rank_in
    outbox = (
        jnp.zeros((device_count * slot_cap, row_width), latents.dtype).at[send_slot].set(latents)
    )
    labels = jnp.full((device_count * slot_cap,), row_count, jnp.int32).at[send_slot].set(local_row)
    inbox_rows, inbox_labels = (
        lax.all_to_all(
            outbox.reshape(device_count, slot_cap, row_width),
            ("seq", "tile"),
            split_axis=0,
            concat_axis=0,
            tiled=True,
        ),
        lax.all_to_all(
            labels.reshape(device_count, slot_cap),
            ("seq", "tile"),
            split_axis=0,
            concat_axis=0,
            tiled=True,
        ),
    )
    grid_rows = (
        jnp.zeros((row_count, row_width), jnp.bfloat16)
        .at[inbox_labels.reshape(-1)]
        .set(inbox_rows.reshape(-1, row_width), mode="drop")
    )
    grid_latent = grid_rows.reshape(FS, TH, W * LAT)
    extended = extended_2(grid_latent, (("tile", 1),), 1)
    before = from_behind(extended, "seq", 1)
    window_in = jnp.concatenate([before, extended], axis=0).reshape(FS + 2, TH + 2, W, LAT)
    window_in = jnp.pad(window_in, ((0, 0), (0, 0), (1, 1), (0, 0)))
    first_conv = causal_taps(window_in, w_in, b_in)
    first_act = normed_silu(first_conv, gain_in)
    act_ext = extended_2(first_act.reshape(FS, TH, W * C1), (("tile", 1),), 1)
    act_ext = jnp.pad(act_ext.reshape(FS, TH + 2, W, C1), ((0, 0), (0, 0), (1, 1), (0, 0)))
    section_out = upsample_conv(act_ext, w_up, b_up)
    upsampled = lax.all_to_all(
        section_out.reshape(FS, 2 * TH, 2 * W * C2), "seq", split_axis=2, concat_axis=0, tiled=True
    )
    upsampled = upsampled.reshape(FS * seq_count, 2 * TH, 2 * W // seq_count, C2)
    res_act = normed_silu(upsampled.astype(jnp.float32), gain_res)
    res_ext = extended_2(res_act, (("seq", 2), ("tile", 1)), 1)
    res_ext = jnp.pad(res_ext, ((2, 0), (0, 0), (0, 0), (0, 0)))
    res_conv = causal_taps(res_ext, w_res, b_res)
    decoded = (upsampled.astype(jnp.float32) + res_conv).astype(jnp.bfloat16)
    return decoded.reshape(decoded.shape[0], 2 * TH, -1)


def solution(mesh):
    return jax.shard_map(
        local,
        mesh=mesh,
        in_specs=(
            P(("seq", "tile"), None),
            P(("seq", "tile")),
            P(),
            P(),
            P(),
            P(),
            P(),
            P(),
            P(),
            P(),
        ),
        out_specs=P(None, "tile", "seq"),
        check_vma=False,
    )
```

profile of v0, /device:TPU:7, one launch (start us, length us, event | category | flops | bytes accessed | tf_op | source)
XLA Modules:
  0.0 614.1 jit_solution(8333284277565260925)
XLA Ops:
  2.9 10.8 %all-to-all-start = ((s32[128,1,2]{2,1,0:T(1,128)}), s32[128,1,2]{2,1,0:T(1,128)S(1)}, u32[]{:S(2)}, u32[]{:S(2)}) async-start(s32[128,1,2]{2,1,0:T(1,128)} %bitcast), calls=%async_computation | async-start | bytes 131072 | tf_op jit(solution)/shard_map/all_to_all | solution.py:116
  15.4 6.2 %all-to-all-done = s32[128,1,2]{2,1,0:T(1,128)S(1)} async-done(((s32[128,1,2]{2,1,0:T(1,128)}), s32[128,1,2]{2,1,0:T(1,128)S(1)}, u32[]{:S(2)}, u32[]{:S(2)}) %all-to-all-start) | async-done | bytes 1056 | tf_op jit(solution)/shard_map/all_to_all | solution.py:116
  29.1 6.5 %all-to-all-done.1 = bf16[128,2,128]{2,1,0:T(2,128)(2,1)S(1)} async-done(((bf16[128,2,128]{2,1,0:T(2,128)(2,1)}), bf16[128,2,128]{2,1,0:T(2,128)(2,1)S(1)}, u32[]{:S(2)}, u32[]{:S(2)}) %all-to-all-start.1) | async-done | bytes 65568 | tf_op jit(solution)/shard_map/all_to_all | solution.py:109
  102.5 6.5 %collective-permute-start.3 = (bf16[2,1,49152]{2,0,1:T(2,128)(2,1)S(1)}, bf16[2,1,49152]{2,0,1:T(2,128)(2,1)S(1)}, u32[]{:S(2)}, u32[]{:S(2)}) collective-permute-start(bf16[2,1,49152]{2,0,1:T(2,128)(2,1)S(1)} %get-tuple-element.44), channel_id=1, source_target_pairs={{0,1},{1,2},{2,3},{3,4},{4,5},{5,6},{6,7},{7,8},{8,9},{9,10},{10,1... | collective-permute-start | bytes 589832 | tf_op jit(solution)/shard_map/ppermute | solution.py:19
  119.1 20.7 %fusion.57 = (bf16[2,8,256,384]{3,0,2,1:T(2,128)(2,1)S(1)}, bf16[2,8,256,384]{3,0,2,1:T(2,128)(2,1)}, bf16[2,8,256,384]{3,0,2,1:T(2,128)(2,1)}, bf16[2,8,256,384...) fusion(bf16[2,12,260,384]{3,0,2,1:T(2,128)(2,1)S(1)} %bitcast.103), kind=kLoop, calls=%fused_computation.140 | loop fusion | bytes 56623104 | tf_op jit(solution)/shard_map/slice | solution.py:71
  139.9 30.7 %pad_maximum_fusion = bf16[2,8,256,1152]{3,0,2,1:T(2,128)(2,1)} fusion(bf16[2,8,256,384]{3,0,2,1:T(2,128)(2,1)S(1)} %get-tuple-element.11, bf16[2,8,256,384]{3,0,2,1:T(2,128)(2,1)S(1)} %get-tuple-element.12, bf16[2,8,256,384]{3,0,2,1:T(2,128)(2,1)S(1)} %get-tuple-element.13), kind=kLoop, calls=%fused_computation.3 | loop fusion | flops 28311552 | bytes 18874368 | tf_op jit(solution)/shard_map/concatenate | solution.py:69
  170.6 9.1 %copy.133 = bf16[2,8,256,1152]{3,2,1,0:T(8,128)(2,1)} copy(bf16[2,8,256,1152]{3,0,2,1:T(2,128)(2,1)} %pad_maximum_fusion) | data formatting | bytes 18874368 | tf_op jit(solution)/shard_map/concatenate | solution.py:69
  179.7 13.1 %pad_maximum_fusion.1 = bf16[2,8,256,1152]{3,0,2,1:T(2,128)(2,1)} fusion(bf16[2,8,256,384]{3,0,2,1:T(2,128)(2,1)} %get-tuple-element.8, bf16[2,8,256,384]{3,0,2,1:T(2,128)(2,1)} %get-tuple-element.9, bf16[2,8,256,384]{3,0,2,1:T(2,128)(2,1)} %get-tuple-element.10), kind=kLoop, calls=%fused_computation.4 | loop fusion | flops 28311552 | bytes 18874368 | tf_op jit(solution)/shard_map/concatenate | solution.py:69
  192.7 9.1 %copy.134 = bf16[2,8,256,1152]{3,2,1,0:T(8,128)(2,1)} copy(bf16[2,8,256,1152]{3,0,2,1:T(2,128)(2,1)} %pad_maximum_fusion.1) | data formatting | bytes 18874368 | tf_op jit(solution)/shard_map/concatenate | solution.py:69
  201.8 31.2 %pad_maximum_fusion.2 = bf16[2,8,256,1152]{3,0,2,1:T(2,128)(2,1)} fusion(bf16[2,8,256,384]{3,0,2,1:T(2,128)(2,1)} %get-tuple-element.6, bf16[2,8,256,384]{3,0,2,1:T(2,128)(2,1)} %get-tuple-element.7, bf16[2,8,256,384]{3,0,2,1:T(2,128)(2,1)S(1)} %get-tuple-element.5), kind=kLoop, calls=%fused_computation.5 | loop fusion | flops 28311552 | bytes 18874368 | tf_op jit(solution)/shard_map/concatenate | solution.py:69
  233.1 9.2 %copy.135 = bf16[2,8,256,1152]{3,2,1,0:T(8,128)(2,1)} copy(bf16[2,8,256,1152]{3,0,2,1:T(2,128)(2,1)} %pad_maximum_fusion.2) | data formatting | bytes 18874368 | tf_op jit(solution)/shard_map/concatenate | solution.py:69
  242.3 7.1 %fusion.20 = f32[4096,192]{0,1:T(8,128)S(1)} fusion(bf16[4096,1152]{1,0:T(8,128)(2,1)} %bitcast.119, bf16[3456,192]{0,1:T(8,128)(2,1)S(1)} %copy-done.18), kind=kOutput, calls=%fused_computation.58 | convolution fusion | flops 1811939328 | bytes 13025280 | tf_op jit(solution)/shard_map/dot_general | solution.py:77
  249.4 7.1 %convolution_add_fusion.8 = f32[4096,192]{0,1:T(8,128)S(1)} fusion(f32[4096,192]{0,1:T(8,128)S(1)} %fusion.20, bf16[4096,1152]{1,0:T(8,128)(2,1)} %bitcast.106, bf16[3456,192]{0,1:T(8,128)(2,1)S(1)} %copy-done.18), kind=kOutput, calls=%fused_computation.35 | convolution fusion | flops 1812725760 | bytes 16171008 | tf_op jit(solution)/shard_map/dot_general | solution.py:77
  267.3 44.1 %copy.137 = bf16[2,8,49152]{1,0,2:T(2,128)(2,1)} copy(bf16[2,8,49152]{2,1,0:T(8,128)(2,1)} %reshape_reshape.3) | data formatting | bytes 3145728 | tf_op jit(solution)/shard_map/reshape;reshape | solution.py:140
  311.4 29.3 %reshape.257 = bf16[8,2,49152]{2,1,0:T(2,128)(2,1)S(1)} reshape(bf16[49152,2,8]{2,1,0:T(2,128)(2,1)} %bitcast.104) | data formatting | bytes 3145728
  340.7 24.8 %all_to_all.23 = bf16[8,2,49152]{2,1,0:T(2,128)(2,1)S(1)} all-to-all(bf16[8,2,49152]{2,1,0:T(2,128)(2,1)S(1)} %reshape.257), channel_id=1, replica_groups=mesh['seq'=8,'tile'=16] {'seq'}, dimensions={0} | all-to-all | bytes 3145728 | tf_op jit(solution)/shard_map/all_to_all | solution.py:139
  365.5 31.8 %reshape.258 = bf16[49152,2,8]{2,1,0:T(2,128)(2,1)} reshape(bf16[8,2,49152]{2,1,0:T(2,128)(2,1)S(1)} %all_to_all.23) | data formatting | bytes 3145728
  397.3 45.4 %copy.138 = bf16[2,8,49152]{2,1,0:T(8,128)(2,1)S(1)} copy(bf16[2,8,49152]{1,0,2:T(2,128)(2,1)} %bitcast.105) | data formatting | bytes 3145728 | tf_op jit(solution)/shard_map/all_to_all | solution.py:139
  461.5 6.2 %collective-permute-start.7 = (bf16[16,1,34,192]{3,2,1,0:T(8,128)(2,1)S(1)}, bf16[16,1,34,192]{3,2,1,0:T(8,128)(2,1)S(1)}, u32[]{:S(2)}, u32[]{:S(2)}) collective-permute-start(bf16[16,1,34,192]{3,2,1,0:T(8,128)(2,1)S(1)} %get-tuple-element.40), channel_id=1, source_target_pairs={{0,1},{1,2},{2,3},{3,4},{4,5},{5,6},{6,7},{7,8},{8,9},{9,10},{10,1... | collective-permute-start | bytes 626696 | tf_op jit(solution)/shard_map/ppermute | solution.py:19
  469.7 6.1 fusion.5
  493.6 14.8 %fusion.58 = (bf16[16,8,32,192]{3,2,1,0:T(8,128)(2,1)}, bf16[16,8,32,192]{3,2,1,0:T(8,128)(2,1)}, bf16[16,8,32,192]{3,2,1,0:T(8,128)(2,1)}, bf16[16,8,32,192]{3,...) fusion(bf16[18,10,34,192]{3,2,1,0:T(8,128)(2,1)S(1)} %fusion.12), kind=kLoop, calls=%fused_computation.141 | loop fusion | bytes 56623104 | tf_op jit(solution)/shard_map/slice | solution.py:43
  508.4 7.3 %pad_maximum_fusion.12 = bf16[16,8,32,576]{3,2,1,0:T(8,128)(2,1)} fusion(bf16[16,8,32,192]{3,2,1,0:T(8,128)(2,1)} %get-tuple-element.36, bf16[16,8,32,192]{3,2,1,0:T(8,128)(2,1)} %get-tuple-element.37, bf16[16,8,32,192]{3,2,1,0:T(8,128)(2,1)} %get-tuple-element.35), kind=kLoop, calls=%fused_computation.23 | loop fusion | flops 14155776 | bytes 9437184 | tf_op jit(solution)/shard_map/concatenate | solution.py:41
  515.7 6.2 %fusion.22 = f32[4096,192]{0,1:T(8,128)} fusion(bf16[4096,576]{1,0:T(8,128)(2,1)} %bitcast.114, bf16[5184,192]{0,1:T(8,128)(2,1)} %param.18), kind=kOutput, calls=%fused_computation.72 | convolution fusion | flops 905969664 | bytes 8634368 | tf_op jit(solution)/shard_map/dot_general | solution.py:53
  521.9 6.1 pad_maximum_fusion.5
  (174 shorter events, 223.5 us)
Async XLA Ops:
  2.9 18.7 %all-to-all-start = ((s32[128,1,2]{2,1,0:T(1,128)}), s32[128,1,2]{2,1,0:T(1,128)S(1)}, u32[]{:S(2)}, u32[]{:S(2)}) async-start(s32[128,1,2]{2,1,0:T(1,128)} %bitcast), calls=%async_computation | async-start | bytes 131072 | tf_op jit(solution)/shard_map/all_to_all | solution.py:116
  21.6 14.1 %all-to-all-start.1 = ((bf16[128,2,128]{2,1,0:T(2,128)(2,1)}), bf16[128,2,128]{2,1,0:T(2,128)(2,1)S(1)}, u32[]{:S(2)}, u32[]{:S(2)}) async-start(bf16[128,2,128]{2,1,0:T(2,128)(2,1)} %bitcast.2), calls=%async_computation.1 | async-start | bytes 131072 | tf_op jit(solution)/shard_map/all_to_all | solution.py:109
  36.9 7.4 %collective-permute-start.1 = (bf16[2,1,2048]{2,1,0:T(2,128)(2,1)S(1)}, bf16[2,1,2048]{2,1,0:T(2,128)(2,1)S(1)}, u32[]{:S(2)}, u32[]{:S(2)}) collective-permute-start(bf16[2,1,2048]{2,1,0:T(2,128)(2,1)S(1)} %get-tuple-element.74), channel_id=1, source_target_pairs={{1,0},{2,1},{3,2},{4,3},{5,4},{6,5},{7,6},{8,7},{9,8},{10,9},{11,1... | collective-permute-start | bytes 24584 | tf_op jit(solution)/shard_map/ppermute | solution.py:22
  39.3 5.9 collective-permute-start
  45.2 5.7 collective-permute-start.2
  56.2 6.2 %copy-start.15 = (bf16[2,4,128,16]{3,2,0,1:T(8,128)(2,1)S(1)}, bf16[2,4,128,16]{3,2,0,1:T(8,128)(2,1)}, u32[]{:S(2)}) copy-start(bf16[2,4,128,16]{3,2,0,1:T(8,128)(2,1)} %get-tuple-element.54) | copy-start | bytes 98308
  56.2 6.2 %copy-start.16 = (bf16[2,4,128,16]{3,2,0,1:T(8,128)(2,1)S(1)}, bf16[2,4,128,16]{3,2,0,1:T(8,128)(2,1)}, u32[]{:S(2)}) copy-start(bf16[2,4,128,16]{3,2,0,1:T(8,128)(2,1)} %get-tuple-element.68) | copy-start | bytes 98308
  62.3 9.5 %copy-start.14 = (bf16[2,4,128,16]{3,2,0,1:T(8,128)(2,1)S(1)}, bf16[2,4,128,16]{3,2,0,1:T(8,128)(2,1)}, u32[]{:S(2)}) copy-start(bf16[2,4,128,16]{3,2,0,1:T(8,128)(2,1)} %get-tuple-element.50) | copy-start | bytes 98308
  71.8 9.6 %copy-start.12 = (bf16[2,4,128,16]{3,2,0,1:T(8,128)(2,1)S(1)}, bf16[2,4,128,16]{3,2,0,1:T(8,128)(2,1)}, u32[]{:S(2)}) copy-start(bf16[2,4,128,16]{3,2,0,1:T(8,128)(2,1)} %get-tuple-element.71) | copy-start | bytes 98308
  71.8 9.6 %copy-start.13 = (bf16[2,4,128,16]{3,2,0,1:T(8,128)(2,1)S(1)}, bf16[2,4,128,16]{3,2,0,1:T(8,128)(2,1)}, u32[]{:S(2)}) copy-start(bf16[2,4,128,16]{3,2,0,1:T(8,128)(2,1)} %get-tuple-element.72) | copy-start | bytes 98308
  81.4 6.0 copy-start.21
  95.8 13.2 %copy-start.19 = (f32[384]{0:T(512)S(1)}, f32[384]{0:T(512)}, u32[]{:S(2)}) copy-start(f32[384]{0:T(512)} %param.14) | copy-start | bytes 4612
  100.6 10.5 %collective-permute-start.4 = (bf16[2,1,49152]{2,0,1:T(2,128)(2,1)S(1)}, bf16[2,1,49152]{2,0,1:T(2,128)(2,1)S(1)}, u32[]{:S(2)}, u32[]{:S(2)}) collective-permute-start(bf16[2,1,49152]{2,0,1:T(2,128)(2,1)S(1)} %get-tuple-element.45), channel_id=1, source_target_pairs={{1,0},{2,1},{3,2},{4,3},{5,4},{6,5},{7,6},{8,7},{9,8},{10,9},{11,1... | collective-permute-start | bytes 589832 | tf_op jit(solution)/shard_map/ppermute | solution.py:22
  102.5 10.3 %collective-permute-start.3 = (bf16[2,1,49152]{2,0,1:T(2,128)(2,1)S(1)}, bf16[2,1,49152]{2,0,1:T(2,128)(2,1)S(1)}, u32[]{:S(2)}, u32[]{:S(2)}) collective-permute-start(bf16[2,1,49152]{2,0,1:T(2,128)(2,1)S(1)} %get-tuple-element.44), channel_id=1, source_target_pairs={{0,1},{1,2},{2,3},{3,4},{4,5},{5,6},{6,7},{7,8},{8,9},{9,10},{10,1... | collective-permute-start | bytes 589832 | tf_op jit(solution)/shard_map/ppermute | solution.py:19
  233.0 9.2 %copy-start.18 = (bf16[3456,192]{0,1:T(8,128)(2,1)S(1)}, bf16[3456,192]{0,1:T(8,128)(2,1)}, u32[]{:S(2)}) copy-start(bf16[3456,192]{0,1:T(8,128)(2,1)} %param.15) | copy-start | bytes 3981316
  242.3 14.2 %slice-start = ((s8[9437184]{0:T(1024)(128)(4,1)}), s8[4194304]{0:T(1024)(128)(4,1)S(1)}, s32[]{:S(2)}) async-start(s8[9437184]{0:T(1024)(128)(4,1)} %bitcast.120), calls=%async_computation.3 | async-start | bytes 8388608
  242.3 14.2 %slice-start.1 = ((s8[9437184]{0:T(1024)(128)(4,1)}), s8[4194304]{0:T(1024)(128)(4,1)S(1)}, s32[]{:S(2)}) async-start(s8[9437184]{0:T(1024)(128)(4,1)} %bitcast.120), calls=%async_computation.4 | async-start | bytes 8388608
  249.4 7.1 %slice-start.2 = ((s8[9437184]{0:T(1024)(128)(4,1)}), s8[1048576]{0:T(1024)(128)(4,1)S(1)}, s32[]{:S(2)}) async-start(s8[9437184]{0:T(1024)(128)(4,1)} %bitcast.120), calls=%async_computation.5 | async-start | bytes 2097152
  249.4 7.1 %copy-start.23 = (f32[192]{0:T(256)S(1)}, f32[192]{0:T(256)}, u32[]{:S(2)}) copy-start(f32[192]{0:T(256)} %param.16) | copy-start | bytes 2308
  453.7 6.3 %collective-permute-start.6 = (bf16[16,8,1,192]{3,2,1,0:T(2,128)(2,1)S(1)}, bf16[16,8,1,192]{3,2,1,0:T(2,128)(2,1)S(1)}, u32[]{:S(2)}, u32[]{:S(2)}) collective-permute-start(bf16[16,8,1,192]{3,2,1,0:T(2,128)(2,1)S(1)} %get-tuple-element.43), channel_id=1, source_target_pairs={{16,0},{32,16},{48,32},{64,48},{80,64},{96,80},{112,96},{17,1},{33... | collective-permute-start | bytes 147464 | tf_op jit(solution)/shard_map/ppermute | solution.py:22
  456.6 4.5 collective-permute-start.5
  461.5 14.3 %collective-permute-start.7 = (bf16[16,1,34,192]{3,2,1,0:T(8,128)(2,1)S(1)}, bf16[16,1,34,192]{3,2,1,0:T(8,128)(2,1)S(1)}, u32[]{:S(2)}, u32[]{:S(2)}) collective-permute-start(bf16[16,1,34,192]{3,2,1,0:T(8,128)(2,1)S(1)} %get-tuple-element.40), channel_id=1, source_target_pairs={{0,1},{1,2},{2,3},{3,4},{4,5},{5,6},{6,7},{7,8},{8,9},{9,10},{10,1... | collective-permute-start | bytes 626696 | tf_op jit(solution)/shard_map/ppermute | solution.py:19
  467.7 13.0 %collective-permute-start.8 = (bf16[16,1,34,192]{3,2,1,0:T(8,128)(2,1)S(1)}, bf16[16,1,34,192]{3,2,1,0:T(8,128)(2,1)S(1)}, u32[]{:S(2)}, u32[]{:S(2)}) collective-permute-start(bf16[16,1,34,192]{3,2,1,0:T(8,128)(2,1)S(1)} %get-tuple-element.41), channel_id=1, source_target_pairs={{1,0},{2,1},{3,2},{4,3},{5,4},{6,5},{7,6},{8,7},{9,8},{10,9},{11,1... | collective-permute-start | bytes 626696 | tf_op jit(solution)/shard_map/ppermute | solution.py:22
  515.7 6.2 %copy-start.9 = (bf16[16,8,32,192]{3,2,1,0:T(8,128)(2,1)S(1)}, bf16[16,8,32,192]{3,2,1,0:T(8,128)(2,1)}, u32[]{:S(2)}) copy-start(bf16[16,8,32,192]{3,2,1,0:T(8,128)(2,1)} %get-tuple-element.29) | copy-start | bytes 4718596
  (14 other events, 62.2 us)
where the time goes:
time: 624 us; the launch traced here: 614 us
  local copies, waits for them, and re-layouts  272 us (44%)
  other arithmetic  153 us (25%)
  matrix products  88.2 us (14%)
  starting transfers between devices  50.7 us (8%)
  blocking collectives  24.8 us (4%)
  waiting for transfers between devices  23.7 us (4%)
    concatenate x3, other arithmetic, upsample_conv(): jnp.concatenate([doubled[:, row_off:row_off + height, col_off:col_off + b...  75 us
    dot_general x18, matrix products, causal_taps(): jnp.dot(window.reshape(-1, 3 * channels), weight[start:start + 3 * channe...  69.6 us
    unnamed x60, local copies, waits for them, and re-layouts  64 us
    concatenate x14, other arithmetic, causal_taps(): jnp.concatenate([padded[time_off:time_off + frames, row_off:row_off + hei...  54.5 us
    another operation x2, local copies, waits for them, and re-layouts, local(): section_out.reshape(FS, 2 * TH, 2 * W * C2)  47.3 us
    all_to_all x1, local copies, waits for them, and re-layouts, local(): lax.all_to_all(section_out.reshape(FS, 2 * TH, 2 * W * C2), 'seq', split_...  45.4 us
    concatenate x3, local copies, waits for them, and re-layouts, upsample_conv(): jnp.concatenate([doubled[:, row_off:row_off + height, col_off:col_off + b...  27.4 us
    slice x6, local copies, waits for them, and re-layouts, causal_taps(): padded[time_off:time_off + frames, row_off:row_off + height, col_off:col_...  27.3 us
  transfers between devices with their start and end apart: 11, of which 8 were waited for; matrix products, arithmetic and copies ran while one was open for 2% of the time, Pallas kernels for 0%

commit v1 on v0

--- a/solution.py
+++ b/solution.py
@@ -9,6 +9,18 @@
 FS = 2
 TH = 4
 W = 128
+
+
+def cut_along(value, dim, size):
+    dims = value.shape
+    blocks = value.reshape(*dims[:dim], size, dims[dim] // size, *dims[dim + 1 :])
+    return jnp.moveaxis(blocks, dim, 0)
+
+
+def laid_out(pieces, dim):
+    pieces = jnp.moveaxis(pieces, 0, dim)
+    dims = pieces.shape
+    return pieces.reshape(*dims[:dim], dims[dim] * dims[dim + 1], *dims[dim + 2 :])
 
 
 def extended_2(block, sides, width):
@@ -136,9 +148,15 @@
     act_ext = extended_2(first_act.reshape(FS, TH, W * C1), (("tile", 1),), 1)
     act_ext = jnp.pad(act_ext.reshape(FS, TH + 2, W, C1), ((0, 0), (0, 0), (1, 1), (0, 0)))
     section_out = upsample_conv(act_ext, w_up, b_up)
-    upsampled = lax.all_to_all(
-        section_out.reshape(FS, 2 * TH, 2 * W * C2), "seq", split_axis=2, concat_axis=0, tiled=True
-    )
+    x_2 = section_out.reshape(FS, 2 * TH, 2 * W * C2)
+    count_2, place = (lax.axis_size("seq"), lax.axis_index("seq"))
+    blocks = cut_along(x_2, 2, count_2)
+    outs = [blocks[place]]
+    for step in range(1, count_2):
+        sent = blocks[place ^ step]
+        outs.append(lax.ppermute(sent, "seq", [(i_2, i_2 ^ step) for i_2 in range(count_2)]))
+    blocks = jnp.stack(outs)[place ^ jnp.arange(count_2)]
+    upsampled = laid_out(blocks, 0)
     upsampled = upsampled.reshape(FS * seq_count, 2 * TH, 2 * W // seq_count, C2)
     res_act = normed_silu(upsampled.astype(jnp.float32), gain_res)
     res_ext = extended_2(res_act, (("seq", 2), ("tile", 1)), 1)

time: 624 us -> 470 us (0.75)
  local copies, waits for them, and re-layouts: 272 us -> 124 us
  blocking collectives: 24.8 us -> 0 us
  waiting for transfers between devices: 23.7 us -> 40.2 us
  starting transfers between devices: 50.7 us -> 60.1 us
    unnamed x60 -> x71, local copies, waits for them, and re-layouts: 64 us -> 2.94 us
    all_to_all x1 -> x0, local copies, waits for them, and re-layouts: 45.4 us -> none  [local(): lax.all_to_all(section_out.reshape(FS, 2 * TH, 2 * W * C2), 'seq', split_...]
    another operation x2 -> x3, local copies, waits for them, and re-layouts: 47.3 us -> 7.09 us  [the longest x1 3.66 us: cut_along(): value.reshape(*dims[:dim], size, dims[dim] // size, *dims[dim + 1:])]
    all_to_all x1 -> x0, blocking collectives: 24.8 us -> none  [local(): lax.all_to_all(section_out.reshape(FS, 2 * TH, 2 * W * C2), 'seq', split_...]
    ppermute x0 -> x7, waiting for transfers between devices: none -> 17 us  [local(): lax.ppermute(sent, 'seq', [(i_2, i_2 ^ step) for i_2 in range(count_2)])]
    ppermute x0 -> x7, starting transfers between devices: none -> 9.32 us  [local(): lax.ppermute(sent, 'seq', [(i_2, i_2 ^ step) for i_2 in range(count_2)])]
  transfers between devices with their start and end apart: 11 -> 18, of which waited for: 8 -> 13; matrix products, arithmetic and copies ran while one was open for 2% -> 3% of each run, Pallas kernels for 0% -> 0%
where the time goes in v1:
time: 470 us; the launch traced here: 465 us
  other arithmetic  153 us (33%)
  local copies, waits for them, and re-layouts  124 us (26%)
  matrix products  86.7 us (18%)
  starting transfers between devices  60.1 us (13%)
  waiting for transfers between devices  40.2 us (9%)
    concatenate x3, other arithmetic, upsample_conv(): jnp.concatenate([doubled[:, row_off:row_off + height, col_off:col_off + b...  74.8 us
    dot_general x18, matrix products, causal_taps(): jnp.dot(window.reshape(-1, 3 * channels), weight[start:start + 3 * channe...  69.2 us
    concatenate x14, other arithmetic, causal_taps(): jnp.concatenate([padded[time_off:time_off + frames, row_off:row_off + hei...  54.1 us
    concatenate x3, local copies, waits for them, and re-layouts, upsample_conv(): jnp.concatenate([doubled[:, row_off:row_off + height, col_off:col_off + b...  27.5 us
    slice x6, local copies, waits for them, and re-layouts, causal_taps(): padded[time_off:time_off + frames, row_off:row_off + height, col_off:col_...  27.3 us
    ppermute x4, starting transfers between devices, extended_2(): lax.ppermute(lax.slice_in_dim(block, block.shape[dim] - width, None, axis...  21.3 us
    slice x1, local copies, waits for them, and re-layouts, upsample_conv(): doubled[:, row_off:row_off + height, col_off:col_off + breadth]  20.8 us
    dot_general x3, matrix products, upsample_conv(): jnp.dot(window.reshape(-1, 3 * channels), weight[start:start + 3 * channe...  17.4 us
  transfers between devices with their start and end apart: 18, of which 13 were waited for; matrix products, arithmetic and copies ran while one was open for 3% of the time, Pallas kernels for 0%

profile of v1, /device:TPU:7, one launch (start us, length us, event | category | flops | bytes accessed | tf_op | source)
XLA Modules:
  0.0 465.2 jit_solution(6305916066521335721)
XLA Ops:
  2.9 10.8 %all-to-all-start = ((s32[128,1,2]{2,1,0:T(1,128)}), s32[128,1,2]{2,1,0:T(1,128)S(1)}, u32[]{:S(2)}, u32[]{:S(2)}) async-start(s32[128,1,2]{2,1,0:T(1,128)} %bitcast), calls=%async_computation | async-start | bytes 131072 | tf_op jit(solution)/shard_map/all_to_all | solution.py:128
  15.4 6.2 %all-to-all-done = s32[128,1,2]{2,1,0:T(1,128)S(1)} async-done(((s32[128,1,2]{2,1,0:T(1,128)}), s32[128,1,2]{2,1,0:T(1,128)S(1)}, u32[]{:S(2)}, u32[]{:S(2)}) %all-to-all-start) | async-done | bytes 1056 | tf_op jit(solution)/shard_map/all_to_all | solution.py:128
  21.6 6.1 %all-to-all-start.1 = ((bf16[128,2,128]{2,1,0:T(2,128)(2,1)}), bf16[128,2,128]{2,1,0:T(2,128)(2,1)S(1)}, u32[]{:S(2)}, u32[]{:S(2)}) async-start(bf16[128,2,128]{2,1,0:T(2,128)(2,1)} %bitcast.2), calls=%async_computation.1 | async-start | bytes 131072 | tf_op jit(solution)/shard_map/all_to_all | solution.py:121
  29.1 6.5 %all-to-all-done.1 = bf16[128,2,128]{2,1,0:T(2,128)(2,1)S(1)} async-done(((bf16[128,2,128]{2,1,0:T(2,128)(2,1)}), bf16[128,2,128]{2,1,0:T(2,128)(2,1)S(1)}, u32[]{:S(2)}, u32[]{:S(2)}) %all-to-all-start.1) | async-done | bytes 65568 | tf_op jit(solution)/shard_map/all_to_all | solution.py:121
  102.7 6.5 %collective-permute-start.3 = (bf16[2,1,49152]{2,0,1:T(2,128)(2,1)S(1)}, bf16[2,1,49152]{2,0,1:T(2,128)(2,1)S(1)}, u32[]{:S(2)}, u32[]{:S(2)}) collective-permute-start(bf16[2,1,49152]{2,0,1:T(2,128)(2,1)S(1)} %get-tuple-element.52), channel_id=1, source_target_pairs={{0,1},{1,2},{2,3},{3,4},{4,5},{5,6},{6,7},{7,8},{8,9},{9,10},{10,1... | collective-permute-start | bytes 589832 | tf_op jit(solution)/shard_map/ppermute | solution.py:31
  119.3 20.8 %fusion.58 = (bf16[2,8,256,384]{3,0,2,1:T(2,128)(2,1)S(1)}, bf16[2,8,256,384]{3,0,2,1:T(2,128)(2,1)}, bf16[2,8,256,384]{3,0,2,1:T(2,128)(2,1)}, bf16[2,8,256,384...) fusion(bf16[2,12,260,384]{3,0,2,1:T(2,128)(2,1)S(1)} %bitcast.130), kind=kLoop, calls=%fused_computation.166 | loop fusion | bytes 56623104 | tf_op jit(solution)/shard_map/slice | solution.py:83
  140.1 30.7 %pad_maximum_fusion = bf16[2,8,256,1152]{3,0,2,1:T(2,128)(2,1)} fusion(bf16[2,8,256,384]{3,0,2,1:T(2,128)(2,1)S(1)} %get-tuple-element.11, bf16[2,8,256,384]{3,0,2,1:T(2,128)(2,1)S(1)} %get-tuple-element.12, bf16[2,8,256,384]{3,0,2,1:T(2,128)(2,1)S(1)} %get-tuple-element.13), kind=kLoop, calls=%fused_computation.4 | loop fusion | flops 28311552 | bytes 18874368 | tf_op jit(solution)/shard_map/concatenate | solution.py:81
  170.8 9.1 %copy.102 = bf16[2,8,256,1152]{3,2,1,0:T(8,128)(2,1)} copy(bf16[2,8,256,1152]{3,0,2,1:T(2,128)(2,1)} %pad_maximum_fusion) | data formatting | bytes 18874368 | tf_op jit(solution)/shard_map/concatenate | solution.py:81
  179.9 13.0 %pad_maximum_fusion.1 = bf16[2,8,256,1152]{3,0,2,1:T(2,128)(2,1)} fusion(bf16[2,8,256,384]{3,0,2,1:T(2,128)(2,1)} %get-tuple-element.8, bf16[2,8,256,384]{3,0,2,1:T(2,128)(2,1)} %get-tuple-element.9, bf16[2,8,256,384]{3,0,2,1:T(2,128)(2,1)} %get-tuple-element.10), kind=kLoop, calls=%fused_computation.5 | loop fusion | flops 28311552 | bytes 18874368 | tf_op jit(solution)/shard_map/concatenate | solution.py:81
  192.9 9.1 %copy.103 = bf16[2,8,256,1152]{3,2,1,0:T(8,128)(2,1)} copy(bf16[2,8,256,1152]{3,0,2,1:T(2,128)(2,1)} %pad_maximum_fusion.1) | data formatting | bytes 18874368 | tf_op jit(solution)/shard_map/concatenate | solution.py:81
  202.1 31.1 %pad_maximum_fusion.2 = bf16[2,8,256,1152]{3,0,2,1:T(2,128)(2,1)} fusion(bf16[2,8,256,384]{3,0,2,1:T(2,128)(2,1)} %get-tuple-element.6, bf16[2,8,256,384]{3,0,2,1:T(2,128)(2,1)} %get-tuple-element.7, bf16[2,8,256,384]{3,0,2,1:T(2,128)(2,1)S(1)} %get-tuple-element.5), kind=kLoop, calls=%fused_computation.6 | loop fusion | flops 28311552 | bytes 18874368 | tf_op jit(solution)/shard_map/concatenate | solution.py:81
  233.2 9.2 %copy.104 = bf16[2,8,256,1152]{3,2,1,0:T(8,128)(2,1)} copy(bf16[2,8,256,1152]{3,0,2,1:T(2,128)(2,1)} %pad_maximum_fusion.2) | data formatting | bytes 18874368 | tf_op jit(solution)/shard_map/concatenate | solution.py:81
  242.4 7.1 %fusion.20 = f32[4096,192]{0,1:T(8,128)S(1)} fusion(bf16[4096,1152]{1,0:T(8,128)(2,1)} %bitcast.143, bf16[3456,192]{0,1:T(8,128)(2,1)S(1)} %copy-done.18), kind=kOutput, calls=%fused_computation.58 | convolution fusion | flops 1811939328 | bytes 13025280 | tf_op jit(solution)/shard_map/dot_general | solution.py:89
  249.6 7.1 %convolution_add_fusion.8 = f32[4096,192]{0,1:T(8,128)S(1)} fusion(f32[4096,192]{0,1:T(8,128)S(1)} %fusion.20, bf16[4096,1152]{1,0:T(8,128)(2,1)} %bitcast.131, bf16[3456,192]{0,1:T(8,128)(2,1)S(1)} %copy-done.18), kind=kOutput, calls=%fused_computation.36 | convolution fusion | flops 1812725760 | bytes 16171008 | tf_op jit(solution)/shard_map/dot_general | solution.py:89
  314.0 6.2 %collective-permute-start.14 = (bf16[16,1,34,192]{3,2,1,0:T(8,128)(2,1)S(1)}, bf16[16,1,34,192]{3,2,1,0:T(8,128)(2,1)S(1)}, u32[]{:S(2)}, u32[]{:S(2)}) collective-permute-start(bf16[16,1,34,192]{3,2,1,0:T(8,128)(2,1)S(1)} %get-tuple-element.40), channel_id=1, source_target_pairs={{0,1},{1,2},{2,3},{3,4},{4,5},{5,6},{6,7},{7,8},{8,9},{9,10},{10,1... | collective-permute-start | bytes 626696 | tf_op jit(solution)/shard_map/ppermute | solution.py:31
  322.2 5.7 %fusion.5 = bf16[16,8,32,576]{3,2,1,0:T(8,128)(2,1)S(1)} fusion(bf16[16,8,1,192]{3,2,1,0:T(2,128)(2,1)S(1)} %collective-permute-done.13, bf16[16,8,32,192]{3,2,1,0:T(8,128)(2,1)S(1)} %multiply_convert_fusion, bf16[16,8,1,192]{3,2,1,0:T(2,128)(2,1)S(1)} %collective-permute-done.12), kind=kLoop, calls=%fused_computation.14 | loop fusion | flops 23592960 | bytes 6389760 | tf_op jit(solution)/shard_map/concatenate | solution.py:53
  345.2 14.7 %fusion.59 = (bf16[16,8,32,192]{3,2,1,0:T(8,128)(2,1)}, bf16[16,8,32,192]{3,2,1,0:T(8,128)(2,1)}, bf16[16,8,32,192]{3,2,1,0:T(8,128)(2,1)}, bf16[16,8,32,192]{3,...) fusion(bf16[18,10,34,192]{3,2,1,0:T(8,128)(2,1)S(1)} %fusion.12), kind=kLoop, calls=%fused_computation.167 | loop fusion | bytes 56623104 | tf_op jit(solution)/shard_map/slice | solution.py:55
  359.9 7.3 %pad_maximum_fusion.12 = bf16[16,8,32,576]{3,2,1,0:T(8,128)(2,1)} fusion(bf16[16,8,32,192]{3,2,1,0:T(8,128)(2,1)} %get-tuple-element.36, bf16[16,8,32,192]{3,2,1,0:T(8,128)(2,1)} %get-tuple-element.37, bf16[16,8,32,192]{3,2,1,0:T(8,128)(2,1)} %get-tuple-element.35), kind=kLoop, calls=%fused_computation.24 | loop fusion | flops 14155776 | bytes 9437184 | tf_op jit(solution)/shard_map/concatenate | solution.py:53
  367.3 6.3 %fusion.22 = f32[4096,192]{0,1:T(8,128)} fusion(bf16[4096,576]{1,0:T(8,128)(2,1)} %bitcast.139, bf16[5184,192]{0,1:T(8,128)(2,1)} %param.18), kind=kOutput, calls=%fused_computation.72 | convolution fusion | flops 905969664 | bytes 8634368 | tf_op jit(solution)/shard_map/dot_general | solution.py:65
  373.5 6.2 %pad_maximum_fusion.5 = bf16[16,8,32,576]{3,2,1,0:T(8,128)(2,1)} fusion(bf16[16,8,32,192]{3,2,1,0:T(8,128)(2,1)S(1)} %get-tuple-element.28, bf16[16,8,32,192]{3,2,1,0:T(8,128)(2,1)S(1)} %copy-done.9, bf16[16,8,32,192]{3,2,1,0:T(8,128)(2,1)} %get-tuple-element.30), kind=kLoop, calls=%fused_computation.17 | loop fusion | flops 14155776 | bytes 9437184 | tf_op jit(solution)/shard_map/concatenate | solution.py:53
  379.7 6.0 %fusion.31 = f32[4096,192]{0,1:T(8,128)} fusion(bf16[4096,576]{1,0:T(8,128)(2,1)} %bitcast.140, bf16[5184,192]{0,1:T(8,128)(2,1)} %param.18), kind=kOutput, calls=%fused_computation.81 | convolution fusion | flops 905969664 | bytes 8634368 | tf_op jit(solution)/shard_map/dot_general | solution.py:65
  394.4 5.9 %convolution_add_fusion.6 = f32[4096,192]{0,1:T(8,128)} fusion(f32[4096,192]{0,1:T(8,128)} %fusion.31, bf16[4096,576]{1,0:T(8,128)(2,1)S(1)} %bitcast.133, bf16[5184,192]{0,1:T(8,128)(2,1)} %param.18), kind=kOutput, calls=%fused_computation.31 | convolution fusion | flops 906756096 | bytes 11255808 | tf_op jit(solution)/shard_map/dot_general | solution.py:65
  404.8 5.7 %convolution_add_fusion.5 = f32[4096,192]{0,1:T(8,128)} fusion(f32[4096,192]{0,1:T(8,128)} %convolution_add_fusion.6, bf16[4096,576]{1,0:T(8,128)(2,1)S(1)} %bitcast.134, bf16[5184,192]{0,1:T(8,128)(2,1)} %param.18), kind=kOutput, calls=%fused_computation.30 | convolution fusion | flops 906756096 | bytes 11255808 | tf_op jit(solution)/shard_map/dot_general | solution.py:65
  425.1 5.7 %convolution_add_fusion.3 = f32[4096,192]{0,1:T(8,128)} fusion(f32[4096,192]{0,1:T(8,128)} %convolution_add_fusion.4, bf16[4096,576]{1,0:T(8,128)(2,1)S(1)} %bitcast.136, bf16[5184,192]{0,1:T(8,128)(2,1)} %param.18), kind=kOutput, calls=%fused_computation.28 | convolution fusion | flops 906756096 | bytes 11255808 | tf_op jit(solution)/shard_map/dot_general | solution.py:65
  (200 shorter events, 220.8 us)
Async XLA Ops:
  2.9 18.7 %all-to-all-start = ((s32[128,1,2]{2,1,0:T(1,128)}), s32[128,1,2]{2,1,0:T(1,128)S(1)}, u32[]{:S(2)}, u32[]{:S(2)}) async-start(s32[128,1,2]{2,1,0:T(1,128)} %bitcast), calls=%async_computation | async-start | bytes 131072 | tf_op jit(solution)/shard_map/all_to_all | solution.py:128
  21.6 14.1 %all-to-all-start.1 = ((bf16[128,2,128]{2,1,0:T(2,128)(2,1)}), bf16[128,2,128]{2,1,0:T(2,128)(2,1)S(1)}, u32[]{:S(2)}, u32[]{:S(2)}) async-start(bf16[128,2,128]{2,1,0:T(2,128)(2,1)} %bitcast.2), calls=%async_computation.1 | async-start | bytes 131072 | tf_op jit(solution)/shard_map/all_to_all | solution.py:121
  36.9 7.4 %collective-permute-start.1 = (bf16[2,1,2048]{2,1,0:T(2,128)(2,1)S(1)}, bf16[2,1,2048]{2,1,0:T(2,128)(2,1)S(1)}, u32[]{:S(2)}, u32[]{:S(2)}) collective-permute-start(bf16[2,1,2048]{2,1,0:T(2,128)(2,1)S(1)} %get-tuple-element.82), channel_id=1, source_target_pairs={{1,0},{2,1},{3,2},{4,3},{5,4},{6,5},{7,6},{8,7},{9,8},{10,9},{11,1... | collective-permute-start | bytes 24584 | tf_op jit(solution)/shard_map/ppermute | solution.py:34
  39.3 5.8 %collective-permute-start = (bf16[2,1,2048]{2,1,0:T(2,128)(2,1)S(1)}, bf16[2,1,2048]{2,1,0:T(2,128)(2,1)S(1)}, u32[]{:S(2)}, u32[]{:S(2)}) collective-permute-start(bf16[2,1,2048]{2,1,0:T(2,128)(2,1)S(1)} %get-tuple-element.81), channel_id=1, source_target_pairs={{0,1},{1,2},{2,3},{3,4},{4,5},{5,6},{6,7},{7,8},{8,9},{9,10},{10,1... | collective-permute-start | bytes 24584 | tf_op jit(solution)/shard_map/ppermute | solution.py:31
  45.2 5.8 %collective-permute-start.2 = (bf16[2,6,2048]{2,1,0:T(8,128)(2,1)S(1)}, bf16[2,6,2048]{2,1,0:T(8,128)(2,1)S(1)}, u32[]{:S(2)}, u32[]{:S(2)}) collective-permute-start(bf16[2,6,2048]{2,1,0:T(8,128)(2,1)S(1)} %pad_maximum_fusion.27), channel_id=1, source_target_pairs={{0,16},{16,32},{32,48},{48,64},{64,80},{80,96},{96,112},{1,17},{17... | collective-permute-start | bytes 147464 | tf_op jit(solution)/shard_map/ppermute | solution.py:42
  62.5 9.5 %copy-start.14 = (bf16[2,4,128,16]{3,2,0,1:T(8,128)(2,1)S(1)}, bf16[2,4,128,16]{3,2,0,1:T(8,128)(2,1)}, u32[]{:S(2)}) copy-start(bf16[2,4,128,16]{3,2,0,1:T(8,128)(2,1)} %get-tuple-element.58) | copy-start | bytes 98308
  72.0 9.6 %copy-start.12 = (bf16[2,4,128,16]{3,2,0,1:T(8,128)(2,1)S(1)}, bf16[2,4,128,16]{3,2,0,1:T(8,128)(2,1)}, u32[]{:S(2)}) copy-start(bf16[2,4,128,16]{3,2,0,1:T(8,128)(2,1)} %get-tuple-element.79) | copy-start | bytes 98308
  72.0 9.6 %copy-start.13 = (bf16[2,4,128,16]{3,2,0,1:T(8,128)(2,1)S(1)}, bf16[2,4,128,16]{3,2,0,1:T(8,128)(2,1)}, u32[]{:S(2)}) copy-start(bf16[2,4,128,16]{3,2,0,1:T(8,128)(2,1)} %get-tuple-element.80) | copy-start | bytes 98308
  96.0 13.2 %copy-start.19 = (f32[384]{0:T(512)S(1)}, f32[384]{0:T(512)}, u32[]{:S(2)}) copy-start(f32[384]{0:T(512)} %param.14) | copy-start | bytes 4612
  100.8 10.5 %collective-permute-start.4 = (bf16[2,1,49152]{2,0,1:T(2,128)(2,1)S(1)}, bf16[2,1,49152]{2,0,1:T(2,128)(2,1)S(1)}, u32[]{:S(2)}, u32[]{:S(2)}) collective-permute-start(bf16[2,1,49152]{2,0,1:T(2,128)(2,1)S(1)} %get-tuple-element.53), channel_id=1, source_target_pairs={{1,0},{2,1},{3,2},{4,3},{5,4},{6,5},{7,6},{8,7},{9,8},{10,9},{11,1... | collective-permute-start | bytes 589832 | tf_op jit(solution)/shard_map/ppermute | solution.py:34
  102.7 10.4 %collective-permute-start.3 = (bf16[2,1,49152]{2,0,1:T(2,128)(2,1)S(1)}, bf16[2,1,49152]{2,0,1:T(2,128)(2,1)S(1)}, u32[]{:S(2)}, u32[]{:S(2)}) collective-permute-start(bf16[2,1,49152]{2,0,1:T(2,128)(2,1)S(1)} %get-tuple-element.52), channel_id=1, source_target_pairs={{0,1},{1,2},{2,3},{3,4},{4,5},{5,6},{6,7},{7,8},{8,9},{9,10},{10,1... | collective-permute-start | bytes 589832 | tf_op jit(solution)/shard_map/ppermute | solution.py:31
  242.4 14.2 %slice-start = ((s8[9437184]{0:T(1024)(128)(4,1)}), s8[4194304]{0:T(1024)(128)(4,1)S(1)}, s32[]{:S(2)}) async-start(s8[9437184]{0:T(1024)(128)(4,1)} %bitcast.144), calls=%async_computation.2 | async-start | bytes 8388608
  242.4 14.2 %slice-start.1 = ((s8[9437184]{0:T(1024)(128)(4,1)}), s8[4194304]{0:T(1024)(128)(4,1)S(1)}, s32[]{:S(2)}) async-start(s8[9437184]{0:T(1024)(128)(4,1)} %bitcast.144), calls=%async_computation.3 | async-start | bytes 8388608
  269.7 6.7 %collective-permute-start.5 = (bf16[2,8,6144]{2,1,0:T(8,128)(2,1)S(1)}, bf16[2,8,6144]{2,1,0:T(8,128)(2,1)S(1)}, u32[]{:S(2)}, u32[]{:S(2)}) collective-permute-start(bf16[2,8,6144]{2,1,0:T(8,128)(2,1)S(1)} %bitcast.157), channel_id=1, source_target_pairs={{0,16},{16,0},{32,48},{48,32},{64,80},{80,64},{96,112},{112,96},{1... | collective-permute-start | bytes 589832 | tf_op jit(solution)/shard_map/ppermute | solution.py:157
  270.1 8.0 %collective-permute-start.6 = (bf16[2,8,6144]{2,1,0:T(8,128)(2,1)S(1)}, bf16[2,8,6144]{2,1,0:T(8,128)(2,1)S(1)}, u32[]{:S(2)}, u32[]{:S(2)}) collective-permute-start(bf16[2,8,6144]{2,1,0:T(8,128)(2,1)S(1)} %bitcast.156), channel_id=1, source_target_pairs={{0,32},{16,48},{32,0},{48,16},{64,96},{80,112},{96,64},{112,80},{1... | collective-permute-start | bytes 589832 | tf_op jit(solution)/shard_map/ppermute | solution.py:157
  271.5 10.7 %collective-permute-start.7 = (bf16[2,8,6144]{2,1,0:T(8,128)(2,1)S(1)}, bf16[2,8,6144]{2,1,0:T(8,128)(2,1)S(1)}, u32[]{:S(2)}, u32[]{:S(2)}) collective-permute-start(bf16[2,8,6144]{2,1,0:T(8,128)(2,1)S(1)} %bitcast.155), channel_id=1, source_target_pairs={{0,48},{16,32},{32,16},{48,0},{64,112},{80,96},{96,80},{112,64},{1... | collective-permute-start | bytes 589832 | tf_op jit(solution)/shard_map/ppermute | solution.py:157
  272.6 13.9 %collective-permute-start.8 = (bf16[2,8,6144]{2,1,0:T(8,128)(2,1)S(1)}, bf16[2,8,6144]{2,1,0:T(8,128)(2,1)S(1)}, u32[]{:S(2)}, u32[]{:S(2)}) collective-permute-start(bf16[2,8,6144]{2,1,0:T(8,128)(2,1)S(1)} %bitcast.154), channel_id=1, source_target_pairs={{0,64},{16,80},{32,96},{48,112},{64,0},{80,16},{96,32},{112,48},{1... | collective-permute-start | bytes 589832 | tf_op jit(solution)/shard_map/ppermute | solution.py:157
  274.7 16.2 %collective-permute-start.9 = (bf16[2,8,6144]{2,1,0:T(8,128)(2,1)S(1)}, bf16[2,8,6144]{2,1,0:T(8,128)(2,1)S(1)}, u32[]{:S(2)}, u32[]{:S(2)}) collective-permute-start(bf16[2,8,6144]{2,1,0:T(8,128)(2,1)S(1)} %bitcast.153), channel_id=1, source_target_pairs={{0,80},{16,64},{32,112},{48,96},{64,16},{80,0},{96,48},{112,32},{1... | collective-permute-start | bytes 589832 | tf_op jit(solution)/shard_map/ppermute | solution.py:157
  276.5 15.8 %collective-permute-start.10 = (bf16[2,8,6144]{2,1,0:T(8,128)(2,1)S(1)}, bf16[2,8,6144]{2,1,0:T(8,128)(2,1)S(1)}, u32[]{:S(2)}, u32[]{:S(2)}) collective-permute-start(bf16[2,8,6144]{2,1,0:T(8,128)(2,1)S(1)} %bitcast.152), channel_id=1, source_target_pairs={{0,96},{16,112},{32,64},{48,80},{64,32},{80,48},{96,0},{112,16},{1... | collective-permute-start | bytes 589832 | tf_op jit(solution)/shard_map/ppermute | solution.py:157
  278.2 18.9 %collective-permute-start.11 = (bf16[2,8,6144]{2,1,0:T(8,128)(2,1)S(1)}, bf16[2,8,6144]{2,1,0:T(8,128)(2,1)S(1)}, u32[]{:S(2)}, u32[]{:S(2)}) collective-permute-start(bf16[2,8,6144]{2,1,0:T(8,128)(2,1)S(1)} %bitcast.151), channel_id=1, source_target_pairs={{0,112},{16,96},{32,80},{48,64},{64,48},{80,32},{96,16},{112,0},{1... | collective-permute-start | bytes 589832 | tf_op jit(solution)/shard_map/ppermute | solution.py:157
  306.2 6.3 %collective-permute-start.13 = (bf16[16,8,1,192]{3,2,1,0:T(2,128)(2,1)S(1)}, bf16[16,8,1,192]{3,2,1,0:T(2,128)(2,1)S(1)}, u32[]{:S(2)}, u32[]{:S(2)}) collective-permute-start(bf16[16,8,1,192]{3,2,1,0:T(2,128)(2,1)S(1)} %get-tuple-element.43), channel_id=1, source_target_pairs={{16,0},{32,16},{48,32},{64,48},{80,64},{96,80},{112,96},{17,1},{33... | collective-permute-start | bytes 147464 | tf_op jit(solution)/shard_map/ppermute | solution.py:34
  308.1 5.6 %collective-permute-start.12 = (bf16[16,8,1,192]{3,2,1,0:T(2,128)(2,1)S(1)}, bf16[16,8,1,192]{3,2,1,0:T(2,128)(2,1)S(1)}, u32[]{:S(2)}, u32[]{:S(2)}) collective-permute-start(bf16[16,8,1,192]{3,2,1,0:T(2,128)(2,1)S(1)} %get-tuple-element.42), channel_id=1, source_target_pairs={{0,16},{16,32},{32,48},{48,64},{64,80},{80,96},{96,112},{1,17},{17... | collective-permute-start | bytes 147464 | tf_op jit(solution)/shard_map/ppermute | solution.py:31
  314.0 13.9 %collective-permute-start.14 = (bf16[16,1,34,192]{3,2,1,0:T(8,128)(2,1)S(1)}, bf16[16,1,34,192]{3,2,1,0:T(8,128)(2,1)S(1)}, u32[]{:S(2)}, u32[]{:S(2)}) collective-permute-start(bf16[16,1,34,192]{3,2,1,0:T(8,128)(2,1)S(1)} %get-tuple-element.40), channel_id=1, source_target_pairs={{0,1},{1,2},{2,3},{3,4},{4,5},{5,6},{6,7},{7,8},{8,9},{9,10},{10,1... | collective-permute-start | bytes 626696 | tf_op jit(solution)/shard_map/ppermute | solution.py:31
  320.2 12.1 %collective-permute-start.15 = (bf16[16,1,34,192]{3,2,1,0:T(8,128)(2,1)S(1)}, bf16[16,1,34,192]{3,2,1,0:T(8,128)(2,1)S(1)}, u32[]{:S(2)}, u32[]{:S(2)}) collective-permute-start(bf16[16,1,34,192]{3,2,1,0:T(8,128)(2,1)S(1)} %get-tuple-element.41), channel_id=1, source_target_pairs={{1,0},{2,1},{3,2},{4,3},{5,4},{6,5},{7,6},{8,7},{9,8},{10,9},{11,1... | collective-permute-start | bytes 626696 | tf_op jit(solution)/shard_map/ppermute | solution.py:34
  (21 other events, 113.2 us)
